TPU v7x, 32 devices: a whole 2x2x4 slice. The times are simulated.
32 devices in a mesh: iface: 8 (over z, core), sub: 4 (over y, x).
Axes of the slice: x: 2, y: 2, z: 4, core: 2. Of those that a mesh axis runs over, the one named last changes fastest.
Arguments:
- traces: bfloat16 [8, 32, 256, 256], P('iface', 'sub'), may hold values from -6 to 6
- elem_count: int32 [8, 32], P('iface', 'sub'), may hold values from 16 to 64, as said below
- near_idx: int32 [8, 32, 7], P('iface', 'sub'), may hold values from 0 to 31, as said below
- near_count: int32 [8, 32], P('iface', 'sub'), may hold values from 2 to 7, as said below
- near_blocks: bfloat16 [8, 32, 7, 256, 256], P('iface', 'sub'), may hold values from -0.125 to 0.125
- source_map: bfloat16 [8, 32, 128, 256], P('iface', 'sub'), may hold values from -0.125 to 0.125
- m2l_idx: int32 [8, 4, 3], P('iface', 'sub'), may hold values from 0 to 3, as said below
- m2l_count: int32 [8, 4], P('iface', 'sub'), may hold values from 2 to 3, as said below
- translate: bfloat16 [8, 4, 3, 128, 128], P('iface', 'sub'), may hold values from -0.3125 to 0.3125
- evaluate: bfloat16 [8, 32, 256, 128], P('iface', 'sub'), may hold values from -0.5 to 0.5
- send_idx: int32 [8, 4, 2, 4, 16], P('iface', 'sub'), may hold values from 0 to 511
- recv_idx: int32 [8, 4, 2, 4, 16], P('iface', 'sub'), may hold values from 0 to 511
- recv_count: int32 [8, 4, 2, 4], P('iface', 'sub'), may hold values from 0 to 16, as said below
- couple_weight: float32 [8, 4, 2, 4, 16], P('iface', 'sub'), may hold values from 0.25 to 2
Outputs:
- calderon: bfloat16 [8, 32, 256, 256], P('iface', 'sub')
Inputs may be any that keep to these rules, and one draw needn't show every extreme that they name: `near_idx`: each slot names a leaf of the same cluster at most 3 leaves from its own; slot 0 is the leaf 3 before and slot 1 the leaf 3 after, clipped to the cluster. `near_count`: some leaf of every cluster has all slots live. `elem_count`: some leaf of every cluster is full. `m2l_idx`: the slots of a box name every other box of its cluster once each. `m2l_count`: some box of every cluster has all slots live. `recv_count`: for every receiving box and side, one sending box fills all 16 slots.
All inputs are finite; a program needn't handle non-finite values.
Results may differ from a plain program's by a relative error of at most 0.0044.
Values may be sent and summed in bfloat16 or wider, within the bound.
No kernel may reach another device: no remote copies, remote signals or barrier semaphores. Data moves between devices by JAX's collectives and lax.ppermute only.
A program may use at most 64 MiB of HBM per device.

v0:
```python
import jax
import jax.numpy as jnp
from jax import lax
from jax.sharding import PartitionSpec as P

REACH = 3


def with_halo(block, sides, width):
    for axis, dim in sides:
        count = lax.axis_size(axis)
        forward = [(i, i + 1) for i in range(count - 1)]
        backward = [(target, source) for source, target in forward]
        low = lax.ppermute(
            lax.slice_in_dim(block, block.shape[dim] - width, None, axis=dim), axis, forward
        )
        high = lax.ppermute(lax.slice_in_dim(block, 0, width, axis=dim), axis, backward)
        block = jnp.concatenate([low, block, high], axis=dim)
    return block


def shifted(shard, axis, by):
    count = lax.axis_size(axis)
    pairs = [(i, i + by) for i in range(count) if 0 <= i + by < count]
    return lax.ppermute(shard, axis, pairs)


def shards(
    traces,
    elem_count,
    near_idx,
    near_count,
    near_blocks,
    source_map,
    m2l_idx,
    m2l_count,
    translate,
    evaluate,
    send_idx,
    recv_idx,
    recv_count,
    couple_weight,
):
    leaves_here = traces.shape[1]
    row_count = traces.shape[2]
    leaf_size = row_count // 4
    fields = traces.shape[3]
    positions = jnp.arange(leaf_size, dtype=jnp.int32)
    live_leaf = positions[None, :] < elem_count[0][:, None]
    live_rows = jnp.tile(live_leaf, (1, 4))
    masked = jnp.where(live_rows[:, :, None], traces[0], jnp.zeros((), traces.dtype))
    padded = with_halo(masked, (("sub", 0),), REACH)
    my_index = lax.axis_index("sub")
    local_idx = near_idx[0] - my_index * leaves_here + REACH
    picked = padded[local_idx]
    slot_count = near_idx.shape[2]
    slot_live = jnp.arange(slot_count, dtype=jnp.int32)[None, :] < near_count[0][:, None]
    picked = jnp.where(slot_live[:, :, None, None], picked, jnp.zeros((), picked.dtype))
    near_part = jnp.einsum(
        "lsij,lsjn->lin", near_blocks[0], picked, preferred_element_type=jnp.float32
    )
    moment = jnp.einsum(
        "lqj,ljn->qn", source_map[0], masked, preferred_element_type=jnp.float32
    ).astype(jnp.bfloat16)
    wanted = m2l_idx[0, 0]
    trans_slots = wanted.shape[0]
    all_boxes = lax.all_gather(moment[None], "sub", axis=0, tiled=True)
    chosen = all_boxes[wanted]
    m2l_live = jnp.arange(trans_slots, dtype=jnp.int32) < m2l_count[0, 0]
    chosen = jnp.where(m2l_live[:, None, None], chosen, jnp.zeros((), chosen.dtype))
    box_local = jnp.einsum(
        "mpq,mqn->pn", translate[0, 0], chosen, preferred_element_type=jnp.float32
    ).astype(jnp.bfloat16)
    far_part = jnp.einsum("liq,qn->lin", evaluate[0], box_local, preferred_element_type=jnp.float32)
    element_count = leaves_here * leaf_size
    elements = (
        masked.reshape(leaves_here, 4, leaf_size, fields)
        .transpose(0, 2, 1, 3)
        .reshape(element_count, 4, fields)
    )
    outgoing = elements[send_idx[0, 0]]
    owned = lax.all_to_all(outgoing, "sub", split_axis=1, concat_axis=1, tiled=True)
    from_left = shifted(owned[1], "iface", 1)
    from_right = shifted(owned[0], "iface", -1)
    arrived = jnp.stack([from_left, from_right], axis=0)
    slot_total = recv_idx.shape[4]
    slot_valid = (
        jnp.arange(slot_total, dtype=jnp.int32)[None, None, :] < recv_count[0, 0][:, :, None]
    )
    weights = jnp.where(slot_valid, couple_weight[0, 0], jnp.zeros((), jnp.float32))
    sign_row = jnp.array([1.0, 1.0, -1.0, -1.0], dtype=jnp.float32)
    scaled = arrived.astype(jnp.float32) * weights[..., None, None] * sign_row[:, None]
    targets = recv_idx[0, 0].reshape(-1)
    iface_el = (
        jnp.zeros((element_count, 4, fields), jnp.float32)
        .at[targets]
        .add(scaled.reshape(-1, 4, fields))
    )
    iface_part = (
        iface_el.reshape(leaves_here, leaf_size, 4, fields)
        .transpose(0, 2, 1, 3)
        .reshape(leaves_here, row_count, fields)
    )
    total = near_part + far_part + iface_part
    result = jnp.where(live_rows[:, :, None], total, jnp.zeros((), jnp.float32)).astype(
        jnp.bfloat16
    )
    return result[None]


def solution(mesh):
    return jax.shard_map(
        shards,
        mesh=mesh,
        in_specs=(
            P("iface", "sub", None, None),
            P("iface", "sub"),
            P("iface", "sub", None),
            P("iface", "sub"),
            P("iface", "sub", None, None, None),
            P("iface", "sub", None, None),
            P("iface", "sub", None),
            P("iface", "sub"),
            P("iface", "sub", None, None, None),
            P("iface", "sub", None, None),
            P("iface", "sub", None, None, None),
            P("iface", "sub", None, None, None),
            P("iface", "sub", None, None),
            P("iface", "sub", None, None, None),
        ),
        out_specs=P("iface", "sub", None, None),
        check_vma=False,
    )
```

profile of v0, /device:TPU:1, one launch (start us, length us, event | category | flops | bytes accessed | tf_op | source)
XLA Modules:
  0.0 85.5 jit_solution(13542415011376778090)
XLA Ops:
  0.0 0.8 iota_compare_fusion.2
  0.9 1.5 %copy.37 = bf16[1,8,256,256]{2,3,1,0:T(8,128)(2,1)S(1)} copy(bf16[1,8,256,256]{3,2,1,0:T(8,128)(2,1)} %param.15) | data formatting | bytes 2097152 | tf_op args[0]
  2.5 0.9 %fusion.38 = (bf16[3,256,256]{1,2,0:T(8,128)(2,1)}, bf16[3,256,256]{1,2,0:T(8,128)(2,1)}) fusion(bf16[8,256,256]{1,2,0:T(8,128)(2,1)S(1)} %bitcast_select_fusion), kind=kLoop, calls=%fused_computation.51 | loop fusion | bytes 1572864 | tf_op jit(solution)/shard_map/slice | solution.py:15
  3.4 4.7 %collective-permute-start = (bf16[3,256,256]{1,2,0:T(8,128)(2,1)}, bf16[3,256,256]{1,2,0:T(8,128)(2,1)}, u32[]{:S(2)}, u32[]{:S(2)}) collective-permute-start(bf16[3,256,256]{1,2,0:T(8,128)(2,1)} %get-tuple-element.5), channel_id=1, source_target_pairs={{0,1},{1,2},{2,3},{4,5},{5,6},{6,7},{8,9},{9,10},{10,11},{12,13},{... | collective-permute-start | bytes 1179656 | tf_op jit(solution)/shard_map/ppermute | solution.py:14
  8.1 1.3 %collective-permute-start.1 = (bf16[3,256,256]{1,2,0:T(8,128)(2,1)}, bf16[3,256,256]{1,2,0:T(8,128)(2,1)}, u32[]{:S(2)}, u32[]{:S(2)}) collective-permute-start(bf16[3,256,256]{1,2,0:T(8,128)(2,1)} %get-tuple-element.6), channel_id=1, source_target_pairs={{1,0},{2,1},{3,2},{5,4},{6,5},{7,6},{9,8},{10,9},{11,10},{13,12},{... | collective-permute-start | bytes 1179656 | tf_op jit(solution)/shard_map/ppermute | solution.py:17
  9.7 0.8 copy.42
  10.7 0.8 gather_fusion.2
  11.5 0.8 copy.43
  12.3 4.3 %all-to-all-start = ((bf16[2,4,16,4,256]{4,3,2,0,1:T(4,128)(2,1)}), bf16[2,4,16,4,256]{4,3,2,0,1:T(4,128)(2,1)S(1)}, u32[]{:S(2)}, u32[]{:S(2)}) async-start(bf16[2,4,16,4,256]{4,3,2,0,1:T(4,128)(2,1)} %copy.43), calls=%async_computation | async-start | bytes 524288 | tf_op jit(solution)/shard_map/all_to_all | solution.py:82
  17.4 15.0 %all-gather = bf16[512,256]{0,1:T(8,128)(2,1)S(1)} all-gather(bf16[128,256]{0,1:T(8,128)(2,1)S(1)} %fusion.19), channel_id=2, replica_groups=mesh['iface'=8,'sub'=4] {'sub'}, dimensions={0}, use_global_device_ids=true | all-gather | bytes 327680 | tf_op jit(solution)/shard_map/all_gather | solution.py:67
  33.4 0.6 gather_fusion.1
  34.0 2.1 %fusion.21 = f32[256,8,256]{2,0,1:T(8,128)} fusion(bf16[1,8,256,128]{3,2,1,0:T(8,128)(2,1)S(1)} %copy-done, bf16[3,128,256]{2,1,0:T(8,128)(2,1)S(1)} %gather_fusion.1, pred[3]{0:T(512)(128)(4,1)S(1)} %iota_compare_fusion.3, bf16[1,1,3,128,128]{4,3,2,1,0:T(8,128)(2,1)S(1)} %copy-done.3), kind=kOutput, calls=%fused_computation.23 | convolution fusion | flops 159514624 | bytes 2916355 | tf_op jit(solution)/shard_map/liq,qn->lin/dot_general | solution.py:74
  36.2 4.6 %collective-permute-start.2 = (bf16[4,16,4,256]{3,2,1,0:T(4,128)(2,1)S(1)}, bf16[4,16,4,256]{3,2,1,0:T(4,128)(2,1)S(1)}, u32[]{:S(2)}, u32[]{:S(2)}) collective-permute-start(bf16[4,16,4,256]{3,2,1,0:T(4,128)(2,1)S(1)} %get-tuple-element.7), channel_id=1, source_target_pairs={{0,4},{4,8},{8,12},{12,16},{16,20},{20,24},{24,28},{1,5},{5,9},{9,... | collective-permute-start | bytes 393224 | tf_op jit(solution)/shard_map/ppermute | solution.py:25
  40.8 1.9 %collective-permute-start.3 = (bf16[4,16,4,256]{3,2,1,0:T(4,128)(2,1)S(1)}, bf16[4,16,4,256]{3,2,1,0:T(4,128)(2,1)S(1)}, u32[]{:S(2)}, u32[]{:S(2)}) collective-permute-start(bf16[4,16,4,256]{3,2,1,0:T(4,128)(2,1)S(1)} %get-tuple-element.8), channel_id=1, source_target_pairs={{4,0},{8,4},{12,8},{16,12},{20,16},{24,20},{28,24},{5,1},{9,5},{13... | collective-permute-start | bytes 393224 | tf_op jit(solution)/shard_map/ppermute | solution.py:25
  42.9 4.2 %collective-permute-done.3 = bf16[4,16,4,256]{3,2,1,0:T(4,128)(2,1)S(1)} collective-permute-done((bf16[4,16,4,256]{3,2,1,0:T(4,128)(2,1)S(1)}, bf16[4,16,4,256]{3,2,1,0:T(4,128)(2,1)S(1)}, u32[]{:S(2)}, u32[]{:S(2)}) %collective-permute-start.3) | collective-permute-done | bytes 131104 | tf_op jit(solution)/shard_map/ppermute | solution.py:25
  47.5 1.6 %broadcast_in_dim.80 = f32[512,4,256]{2,1,0:T(4,128)} broadcast(f32[]{:T(128)} %constant.4.clone.1), dimensions={} | broadcast | bytes 2097156 | tf_op jit(solution)/shard_map/broadcast_in_dim | solution.py:95
  49.1 13.6 %scatter_fusion = f32[512,4,256]{2,1,0:T(4,128)} fusion(f32[512,4,256]{2,1,0:T(4,128)} %broadcast_in_dim.80, s32[128]{0:T(128)S(1)} %fusion.34, f32[128,4,256]{2,1,0:T(4,128)S(1)} %fusion.22), kind=kCustom, calls=%fused_computation.3 | custom fusion | flops 131072 | bytes 1573376 | tf_op jit(solution)/shard_map/scatter-add | solution.py:97
  62.7 2.0 %copy.45 = f32[512,4,256]{2,0,1:T(8,128)S(1)} copy(f32[512,4,256]{2,1,0:T(4,128)} %scatter_fusion) | data formatting | bytes 4194304 | tf_op jit(solution)/shard_map/scatter-add | solution.py:97
  64.7 1.5 %copy.46 = f32[8,4,64,256]{3,2,1,0:T(8,128)} copy(f32[8,4,64,256]{3,2,0,1:T(8,128)S(1)} %bitcast.102) | data formatting | bytes 4194304 | tf_op jit(solution)/shard_map/transpose | solution.py:101
  66.2 2.9 %copy.47 = f32[8,256,256]{1,2,0:T(8,128)} copy(f32[8,256,256]{2,1,0:T(8,128)} %bitcast.103) | data formatting | bytes 4194304 | tf_op jit(solution)/shard_map/reshape | solution.py:102
  69.1 1.3 %pad_maximum_fusion = bf16[14,256,256]{1,2,0:T(8,128)(2,1)S(1)} fusion(bf16[3,256,256]{1,2,0:T(8,128)(2,1)} %collective-permute-done.1, bf16[8,256,256]{1,2,0:T(8,128)(2,1)S(1)} %bitcast_select_fusion, bf16[3,256,256]{1,2,0:T(8,128)(2,1)} %collective-permute-done), kind=kLoop, calls=%fused_computation.13 | loop fusion | flops 1835008 | bytes 3670016 | tf_op jit(solution)/shard_map/concatenate | solution.py:18
  70.4 5.2 %gather_fusion = bf16[56,256,256]{1,2,0:T(8,128)(2,1)} fusion(bf16[14,256,256]{1,2,0:T(8,128)(2,1)S(1)} %pad_maximum_fusion, s32[1024]{0:T(1024)S(1)} %pad_clamp_fusion.2), kind=kCustom, calls=%fused_computation | custom fusion | bytes 14680288 | tf_op jit(solution)/shard_map/gather | solution.py:55
  75.6 8.6 %fusion.12 = bf16[1,8,256,256]{2,3,1,0:T(8,128)(2,1)S(1)} fusion(f32[8,256,256]{1,2,0:T(8,128)} %copy.47, f32[256,8,256]{2,0,1:T(8,128)} %fusion.21, bf16[1,8,7,256,256]{4,3,2,1,0:T(8,128)(2,1)} %param.19, bf16[8,7,256,256]{2,3,1,0:T(8,128)(2,1)} %bitcast.104, pred[8,7]{1,0:T(8,128)(4,1)S(1)} %iota_compare_fusion.1, pred[8,256]{1,0:T(8,128)(4,1)S(1)} %tile.9), kind=kOutput, calls=%fused_computation.14 | convolution fusion | flops 1884815360 | bytes 19925048 | tf_op jit(solution)/shard_map/lsij,lsjn->lin/dot_general | solution.py:59
  84.2 1.3 %copy.48 = bf16[1,8,256,256]{3,2,1,0:T(8,128)(2,1)} copy(bf16[1,8,256,256]{2,3,1,0:T(8,128)(2,1)S(1)} %fusion.12) | data formatting | bytes 2097152 | tf_op jit(solution)/shard_map/broadcast_in_dim | solution.py:108
  (55 shorter events, 2.3 us)
Async XLA Ops:
  0.0 34.0 %copy-start = (bf16[1,8,256,128]{3,2,1,0:T(8,128)(2,1)S(1)}, bf16[1,8,256,128]{3,2,1,0:T(8,128)(2,1)}, u32[]{:S(2)}) copy-start(bf16[1,8,256,128]{3,2,1,0:T(8,128)(2,1)} %param.24) | copy-start | bytes 1572868
  2.4 7.0 %copy-start.1 = (bf16[1,8,256,256]{3,2,1,0:T(8,128)(2,1)S(1)}, bf16[1,8,256,256]{3,2,1,0:T(8,128)(2,1)}, u32[]{:S(2)}) copy-start(bf16[1,8,256,256]{3,2,1,0:T(8,128)(2,1)} %param.15) | copy-start | bytes 3145732
  3.4 65.7 %collective-permute-start = (bf16[3,256,256]{1,2,0:T(8,128)(2,1)}, bf16[3,256,256]{1,2,0:T(8,128)(2,1)}, u32[]{:S(2)}, u32[]{:S(2)}) collective-permute-start(bf16[3,256,256]{1,2,0:T(8,128)(2,1)} %get-tuple-element.5), channel_id=1, source_target_pairs={{0,1},{1,2},{2,3},{4,5},{5,6},{6,7},{8,9},{9,10},{10,11},{12,13},{... | collective-permute-start | bytes 1179656 | tf_op jit(solution)/shard_map/ppermute | solution.py:14
  8.1 61.0 %collective-permute-start.1 = (bf16[3,256,256]{1,2,0:T(8,128)(2,1)}, bf16[3,256,256]{1,2,0:T(8,128)(2,1)}, u32[]{:S(2)}, u32[]{:S(2)}) collective-permute-start(bf16[3,256,256]{1,2,0:T(8,128)(2,1)} %get-tuple-element.6), channel_id=1, source_target_pairs={{1,0},{2,1},{3,2},{5,4},{6,5},{7,6},{9,8},{10,9},{11,10},{13,12},{... | collective-permute-start | bytes 1179656 | tf_op jit(solution)/shard_map/ppermute | solution.py:17
  9.5 1.0 %copy-start.6 = (s32[1,1,2,4,16]{4,3,2,1,0:T(4,128)S(1)}, s32[1,1,2,4,16]{4,3,2,1,0:T(4,128)}, u32[]{:S(2)}) copy-start(s32[1,1,2,4,16]{4,3,2,1,0:T(4,128)} %param.25) | copy-start | bytes 1540
  9.7 7.0 %copy-start.8 = (s32[1,1,2,4]{3,2,1,0:T(2,128)S(1)}, s32[1,1,2,4]{3,2,1,0:T(2,128)}, u32[]{:S(2)}) copy-start(s32[1,1,2,4]{3,2,1,0:T(2,128)} %param.27) | copy-start | bytes 100
  9.7 7.1 %copy-start.4 = (f32[1,1,2,4,16]{4,3,2,1,0:T(4,128)S(1)}, f32[1,1,2,4,16]{4,3,2,1,0:T(4,128)}, u32[]{:S(2)}) copy-start(f32[1,1,2,4,16]{4,3,2,1,0:T(4,128)} %param.28) | copy-start | bytes 1540
  9.7 7.2 %copy-start.5 = (s32[1,1,2,4,16]{4,3,2,1,0:T(4,128)S(1)}, s32[1,1,2,4,16]{4,3,2,1,0:T(4,128)}, u32[]{:S(2)}) copy-start(s32[1,1,2,4,16]{4,3,2,1,0:T(4,128)} %param.26) | copy-start | bytes 1540
  9.7 7.3 %copy-start.2 = (bf16[1,8,128,256]{3,2,1,0:T(8,128)(2,1)S(1)}, bf16[1,8,128,256]{3,2,1,0:T(8,128)(2,1)}, u32[]{:S(2)}) copy-start(bf16[1,8,128,256]{3,2,1,0:T(8,128)(2,1)} %param.20) | copy-start | bytes 1572868
  10.5 22.1 %copy-start.10 = (s32[1,1,3]{2,1,0:T(1,128)S(1)}, s32[1,1,3]{2,1,0:T(1,128)}, u32[]{:S(2)}) copy-start(s32[1,1,3]{2,1,0:T(1,128)} %param.21) | copy-start | bytes 40
  10.5 22.8 %copy-start.11 = (s32[1,8]{1,0:T(1,128)S(1)}, s32[1,8]{1,0:T(1,128)}, u32[]{:S(2)}) copy-start(s32[1,8]{1,0:T(1,128)} %param.18) | copy-start | bytes 100
  10.6 22.8 %copy-start.7 = (s32[1,8,7]{1,0,2:T(1,128)S(1)}, s32[1,8,7]{1,0,2:T(1,128)}, u32[]{:S(2)}) copy-start(s32[1,8,7]{1,0,2:T(1,128)} %param.17) | copy-start | bytes 676
  11.5 22.5 %copy-start.3 = (bf16[1,1,3,128,128]{4,3,2,1,0:T(8,128)(2,1)S(1)}, bf16[1,1,3,128,128]{4,3,2,1,0:T(8,128)(2,1)}, u32[]{:S(2)}) copy-start(bf16[1,1,3,128,128]{4,3,2,1,0:T(8,128)(2,1)} %param.23) | copy-start | bytes 294916
  12.3 23.8 %all-to-all-start = ((bf16[2,4,16,4,256]{4,3,2,0,1:T(4,128)(2,1)}), bf16[2,4,16,4,256]{4,3,2,0,1:T(4,128)(2,1)S(1)}, u32[]{:S(2)}, u32[]{:S(2)}) async-start(bf16[2,4,16,4,256]{4,3,2,0,1:T(4,128)(2,1)} %copy.43), calls=%async_computation | async-start | bytes 524288 | tf_op jit(solution)/shard_map/all_to_all | solution.py:82
  33.4 13.9 %copy-start.9 = (f32[4]{0:T(128)S(1)}, f32[4]{0:T(128)}, u32[]{:S(2)}) copy-start(f32[4]{0:T(128)} %constant.6.clone) | copy-start | bytes 52
  36.2 6.7 %collective-permute-start.2 = (bf16[4,16,4,256]{3,2,1,0:T(4,128)(2,1)S(1)}, bf16[4,16,4,256]{3,2,1,0:T(4,128)(2,1)S(1)}, u32[]{:S(2)}, u32[]{:S(2)}) collective-permute-start(bf16[4,16,4,256]{3,2,1,0:T(4,128)(2,1)S(1)} %get-tuple-element.7), channel_id=1, source_target_pairs={{0,4},{4,8},{8,12},{12,16},{16,20},{20,24},{24,28},{1,5},{5,9},{9,... | collective-permute-start | bytes 393224 | tf_op jit(solution)/shard_map/ppermute | solution.py:25
  40.8 6.3 %collective-permute-start.3 = (bf16[4,16,4,256]{3,2,1,0:T(4,128)(2,1)S(1)}, bf16[4,16,4,256]{3,2,1,0:T(4,128)(2,1)S(1)}, u32[]{:S(2)}, u32[]{:S(2)}) collective-permute-start(bf16[4,16,4,256]{3,2,1,0:T(4,128)(2,1)S(1)} %get-tuple-element.8), channel_id=1, source_target_pairs={{4,0},{8,4},{12,8},{16,12},{20,16},{24,20},{28,24},{5,1},{9,5},{13... | collective-permute-start | bytes 393224 | tf_op jit(solution)/shard_map/ppermute | solution.py:25
where the time goes:
time: 86.2 us; the launch traced here: 85.5 us
  local copies, waits for them, and re-layouts  20.9 us (24%)
  starting transfers between devices  16.8 us (19%)
  other arithmetic  16.5 us (19%)
  blocking collectives  15 us (17%)
  matrix products  11.1 us (13%)
  waiting for transfers between devices  4.18 us (5%)
  between operations  0.98 us (1%)
    all_gather x1, blocking collectives, shards(): all_boxes = lax.all_gather(moment[None], 'sub', axis=0, tiled=True)  15 us
    scatter-add x1, other arithmetic, shards(): iface_el = jnp.zeros((element_count, 4, fields), jnp.float32).at[targets]...  13.6 us
    dot_general x1, matrix products, shards(): jnp.einsum('lsij,lsjn->lin', near_blocks[0], picked, preferred_element_ty...  8.57 us
    ppermute x2, starting transfers between devices, shifted(): return lax.ppermute(shard, axis, pairs)  6.51 us
    gather x1, local copies, waits for them, and re-layouts, shards(): picked = padded[local_idx]  5.24 us
    ppermute x1, starting transfers between devices, with_halo(): lax.ppermute(lax.slice_in_dim(block, block.shape[dim] - width, None, axis...  4.69 us
    all_to_all x1, starting transfers between devices, shards(): lax.all_to_all(outgoing, 'sub', split_axis=1, concat_axis=1, tiled=True)  4.32 us
    ppermute x2, waiting for transfers between devices, shifted(): return lax.ppermute(shard, axis, pairs)  4.17 us
  transfers between devices with their start and end apart: 5, of which 1 were waited for; matrix products, arithmetic and copies ran while one was open for 34% of the time, Pallas kernels for 0%

commit v1 on v0

--- a/solution.py
+++ b/solution.py
@@ -79,7 +79,18 @@
         .reshape(element_count, 4, fields)
     )
     outgoing = elements[send_idx[0, 0]]
-    owned = lax.all_to_all(outgoing, "sub", split_axis=1, concat_axis=1, tiled=True)
+    after, b_next = (lax.axis_size("sub"), lax.axis_index("sub"))
+    val = outgoing.shape[1] // after
+    vec_out = list(outgoing.shape)
+    vec_out[1] = val
+    opened = vec_out[1]
+    vec_out[1] = opened * after
+    owned = jnp.zeros(vec_out, outgoing.dtype)
+    for q in range(after):
+        near = lax.dynamic_slice_in_dim(outgoing, (b_next ^ q) * val, val, axis=1)
+        if q:
+            near = lax.ppermute(near, "sub", [(tick, tick ^ q) for tick in range(after)])
+        owned = lax.dynamic_update_slice_in_dim(owned, near, (b_next ^ q) * opened, axis=1)
     from_left = shifted(owned[1], "iface", 1)
     from_right = shifted(owned[0], "iface", -1)
     arrived = jnp.stack([from_left, from_right], axis=0)

time: 86.2 us -> 95.9 us (1.11)
  other arithmetic: 16.5 us -> 21.3 us
  local copies, waits for them, and re-layouts: 20.9 us -> 23.6 us
  matrix products: 11.1 us -> 13 us
    all_to_all x1 -> x0, starting transfers between devices: 4.32 us -> none  [shards(): lax.all_to_all(outgoing, 'sub', split_axis=1, concat_axis=1, tiled=True)]
    ppermute x0 -> x3, starting transfers between devices: none -> 3.28 us  [shards(): lax.ppermute(near, 'sub', [(tick, tick ^ q) for tick in range(after)])]
    dynamic_update_slice x0 -> x3, local copies, waits for them, and re-layouts: none -> 2.64 us  [shards(): lax.dynamic_update_slice_in_dim(owned, near, (b_next ^ q) * opened, axis=1)]
    ppermute x2, starting transfers between devices: 6.51 us -> 8.54 us  [shifted(): return lax.ppermute(shard, axis, pairs)]
    ppermute x1, starting transfers between devices: 4.69 us -> 3.33 us  [with_halo(): lax.ppermute(lax.slice_in_dim(block, block.shape[dim] - width, None, axis...]
    transpose x1, other arithmetic: 0.14 us -> 1.37 us  [shards(): elements = masked.reshape(leaves_here, 4, leaf_size, fields).transpose(0,...]
    lt x1, other arithmetic: 0.07 us -> 1.27 us  [shards(): jnp.arange(slot_count, dtype=jnp.int32)[None, :] < near_count[0][:, None]]
    select_n x1, other arithmetic: 0.01 us -> 1.17 us  [shards(): jnp.where(slot_valid, couple_weight[0, 0], jnp.zeros((), jnp.float32))]
  transfers between devices with their start and end apart: 5 -> 7, of which waited for: 1 -> 1; matrix products, arithmetic and copies ran while one was open for 34% -> 38% of each run, Pallas kernels for 0% -> 0%
where the time goes in v1:
time: 95.9 us; the launch traced here: 94.8 us
  local copies, waits for them, and re-layouts  23.6 us (25%)
  other arithmetic  21.3 us (22%)
  starting transfers between devices  16.4 us (17%)
  blocking collectives  15.3 us (16%)
  matrix products  13 us (14%)
  waiting for transfers between devices  4.18 us (4%)
  between operations  0.98 us (1%)
    all_gather x1, blocking collectives, shards(): all_boxes = lax.all_gather(moment[None], 'sub', axis=0, tiled=True)  15.3 us
    scatter-add x1, other arithmetic, shards(): iface_el = jnp.zeros((element_count, 4, fields), jnp.float32).at[targets]...  13.6 us
    dot_general x1, matrix products, shards(): jnp.einsum('lsij,lsjn->lin', near_blocks[0], picked, preferred_element_ty...  8.56 us
    ppermute x2, starting transfers between devices, shifted(): return lax.ppermute(shard, axis, pairs)  8.54 us
    gather x1, local copies, waits for them, and re-layouts, shards(): picked = padded[local_idx]  5.24 us
    ppermute x2, waiting for transfers between devices, shifted(): return lax.ppermute(shard, axis, pairs)  4.17 us
    ppermute x1, starting transfers between devices, with_halo(): lax.ppermute(lax.slice_in_dim(block, block.shape[dim] - width, None, axis...  3.33 us
    ppermute x3, starting transfers between devices, shards(): lax.ppermute(near, 'sub', [(tick, tick ^ q) for tick in range(after)])  3.28 us
  transfers between devices with their start and end apart: 7, of which 1 were waited for; matrix products, arithmetic and copies ran while one was open for 38% of the time, Pallas kernels for 0%

profile of v1, /device:TPU:1, one launch (start us, length us, event | category | flops | bytes accessed | tf_op | source)
XLA Modules:
  0.0 94.8 jit_solution(1708413624530915024)
XLA Ops:
  0.8 1.4 %select_bitcast_fusion = bf16[8,64,4,256]{3,1,2,0:T(8,128)(2,1)S(1)} fusion(bf16[8,4,64,256]{3,2,1,0:T(8,128)(2,1)} %bitcast.104, pred[8,64]{1,0:T(8,128)(4,1)S(1)} %iota_compare_fusion.2), kind=kLoop, calls=%fused_computation.22 | loop fusion | flops 524288 | bytes 2097664 | tf_op jit(solution)/shard_map/transpose | solution.py:78
  4.9 2.0 %collective-permute-start.2 = (bf16[2,1,16,4,256]{4,3,2,1,0:T(4,128)(2,1)}, bf16[2,1,16,4,256]{4,3,2,1,0:T(4,128)(2,1)}, u32[]{:S(2)}, u32[]{:S(2)}) collective-permute-start(bf16[2,1,16,4,256]{4,3,2,1,0:T(4,128)(2,1)} %get-tuple-element.11), channel_id=1, source_target_pairs={{0,1},{1,0},{2,3},{3,2},{4,5},{5,4},{6,7},{7,6},{8,9},{9,8},{10,11... | collective-permute-start | bytes 196616 | tf_op jit(solution)/shard_map/ppermute | solution.py:92
  6.9 1.2 %collective-permute-start.3 = (bf16[2,1,16,4,256]{4,3,2,1,0:T(4,128)(2,1)}, bf16[2,1,16,4,256]{4,3,2,1,0:T(4,128)(2,1)}, u32[]{:S(2)}, u32[]{:S(2)}) collective-permute-start(bf16[2,1,16,4,256]{4,3,2,1,0:T(4,128)(2,1)} %get-tuple-element.10), channel_id=1, source_target_pairs={{0,2},{1,3},{2,0},{3,1},{4,6},{5,7},{6,4},{7,5},{8,10},{9,11},{10,... | collective-permute-start | bytes 196616 | tf_op jit(solution)/shard_map/ppermute | solution.py:92
  9.0 3.3 %collective-permute-start = (bf16[3,256,256]{1,2,0:T(8,128)(2,1)S(1)}, bf16[3,256,256]{1,2,0:T(8,128)(2,1)S(1)}, u32[]{:S(2)}, u32[]{:S(2)}) collective-permute-start(bf16[3,256,256]{1,2,0:T(8,128)(2,1)S(1)} %get-tuple-element.5), channel_id=1, source_target_pairs={{0,1},{1,2},{2,3},{4,5},{5,6},{6,7},{8,9},{9,10},{10,11},{12,13},{... | collective-permute-start | bytes 1179656 | tf_op jit(solution)/shard_map/ppermute | solution.py:14
  12.3 1.3 %collective-permute-start.1 = (bf16[3,256,256]{1,2,0:T(8,128)(2,1)S(1)}, bf16[3,256,256]{1,2,0:T(8,128)(2,1)}, u32[]{:S(2)}, u32[]{:S(2)}) collective-permute-start(bf16[3,256,256]{1,2,0:T(8,128)(2,1)S(1)} %get-tuple-element.6), channel_id=1, source_target_pairs={{1,0},{2,1},{3,2},{5,4},{6,5},{7,6},{9,8},{10,9},{11,10},{13,12},{... | collective-permute-start | bytes 1179656 | tf_op jit(solution)/shard_map/ppermute | solution.py:17
  15.0 1.5 %fusion.19 = bf16[128,256]{0,1:T(8,128)(2,1)S(1)} fusion(bf16[8,256,256]{1,2,0:T(8,128)(2,1)S(1)} %bitcast_select_fusion, bf16[1,8,128,256]{3,2,1,0:T(8,128)(2,1)} %param.20), kind=kOutput, calls=%fused_computation.19 | convolution fusion | flops 134250496 | bytes 1638400 | tf_op jit(solution)/shard_map/lqj,ljn->qn/dot_general | solution.py:62
  16.5 15.3 %all-gather = bf16[512,256]{0,1:T(8,128)(2,1)S(1)} all-gather(bf16[128,256]{0,1:T(8,128)(2,1)S(1)} %fusion.19), channel_id=2, replica_groups=mesh['iface'=8,'sub'=4] {'sub'}, dimensions={0}, use_global_device_ids=true | all-gather | bytes 327680 | tf_op jit(solution)/shard_map/all_gather | solution.py:67
  33.2 1.3 %iota_compare_fusion.1 = pred[8,7]{1,0:T(8,128)(4,1)} fusion(s32[8]{0:T(128)} %bitcast.111), kind=kLoop, calls=%fused_computation.42 | loop fusion | flops 56 | bytes 88 | tf_op jit(solution)/shard_map/lt | solution.py:57
  35.1 3.0 %fusion.21 = f32[256,8,256]{2,0,1:T(8,128)} fusion(bf16[1,8,256,128]{3,2,1,0:T(8,128)(2,1)S(1)} %copy-done, bf16[3,128,256]{2,1,0:T(8,128)(2,1)S(1)} %gather_fusion.1, pred[3]{0:T(512)(128)(4,1)S(1)} %iota_compare_fusion.3, bf16[1,1,3,128,128]{4,3,2,1,0:T(8,128)(2,1)} %param.23), kind=kOutput, calls=%fused_computation.23 | convolution fusion | flops 159514624 | bytes 2916355 | tf_op jit(solution)/shard_map/liq,qn->lin/dot_general | solution.py:74
  38.1 1.2 %broadcast_select_fusion = f32[128]{0:T(128)} fusion(pred[128]{0:T(512)(128)(4,1)} %lt.160, f32[128]{0:T(128)} %squeeze.47), kind=kLoop, calls=%fused_computation.55 | loop fusion | flops 128 | bytes 1152 | tf_op jit(solution)/shard_map/jit(_where)/select_n | solution.py:101
  39.4 0.9 constant_dynamic-update-slice_fusion.1
  40.2 0.9 constant_dynamic-update-slice_fusion
  42.1 6.6 %collective-permute-start.5 = (bf16[4,16,4,256]{3,2,1,0:T(4,128)(2,1)S(1)}, bf16[4,16,4,256]{3,2,1,0:T(4,128)(2,1)S(1)}, u32[]{:S(2)}, u32[]{:S(2)}) collective-permute-start(bf16[4,16,4,256]{3,2,1,0:T(4,128)(2,1)S(1)} %get-tuple-element.7), channel_id=1, source_target_pairs={{0,4},{4,8},{8,12},{12,16},{16,20},{20,24},{24,28},{1,5},{5,9},{9,... | collective-permute-start | bytes 393224 | tf_op jit(solution)/shard_map/ppermute | solution.py:25
  48.8 1.9 %collective-permute-start.6 = (bf16[4,16,4,256]{3,2,1,0:T(4,128)(2,1)S(1)}, bf16[4,16,4,256]{3,2,1,0:T(4,128)(2,1)S(1)}, u32[]{:S(2)}, u32[]{:S(2)}) collective-permute-start(bf16[4,16,4,256]{3,2,1,0:T(4,128)(2,1)S(1)} %get-tuple-element.8), channel_id=1, source_target_pairs={{4,0},{8,4},{12,8},{16,12},{20,16},{24,20},{28,24},{5,1},{9,5},{13... | collective-permute-start | bytes 393224 | tf_op jit(solution)/shard_map/ppermute | solution.py:25
  50.9 4.2 %collective-permute-done.6 = bf16[4,16,4,256]{3,2,1,0:T(4,128)(2,1)S(1)} collective-permute-done((bf16[4,16,4,256]{3,2,1,0:T(4,128)(2,1)S(1)}, bf16[4,16,4,256]{3,2,1,0:T(4,128)(2,1)S(1)}, u32[]{:S(2)}, u32[]{:S(2)}) %collective-permute-start.6) | collective-permute-done | bytes 131104 | tf_op jit(solution)/shard_map/ppermute | solution.py:25
  56.0 1.6 %broadcast_in_dim.83 = f32[512,4,256]{2,1,0:T(4,128)} broadcast(f32[]{:T(128)} %constant.19.clone.1), dimensions={} | broadcast | bytes 2097156 | tf_op jit(solution)/shard_map/broadcast_in_dim | solution.py:106
  57.7 13.6 %scatter_fusion = f32[512,4,256]{2,1,0:T(4,128)} fusion(f32[512,4,256]{2,1,0:T(4,128)} %broadcast_in_dim.83, s32[128]{0:T(128)S(1)} %fusion.34, f32[128,4,256]{2,1,0:T(4,128)S(1)} %fusion.22), kind=kCustom, calls=%fused_computation.3 | custom fusion | flops 131072 | bytes 1573376 | tf_op jit(solution)/shard_map/scatter-add | solution.py:108
  71.2 2.0 %copy.36 = f32[512,4,256]{2,0,1:T(8,128)S(1)} copy(f32[512,4,256]{2,1,0:T(4,128)} %scatter_fusion) | data formatting | bytes 4194304 | tf_op jit(solution)/shard_map/scatter-add | solution.py:108
  73.2 1.5 %copy.37 = f32[8,4,64,256]{3,2,1,0:T(8,128)} copy(f32[8,4,64,256]{3,2,0,1:T(8,128)S(1)} %bitcast.100) | data formatting | bytes 4194304 | tf_op jit(solution)/shard_map/transpose | solution.py:112
  74.7 2.9 %copy.38 = f32[8,256,256]{1,2,0:T(8,128)} copy(f32[8,256,256]{2,1,0:T(8,128)} %bitcast.101) | data formatting | bytes 4194304 | tf_op jit(solution)/shard_map/reshape | solution.py:113
  78.4 1.3 %pad_maximum_fusion = bf16[14,256,256]{1,2,0:T(8,128)(2,1)S(1)} fusion(bf16[3,256,256]{1,2,0:T(8,128)(2,1)} %collective-permute-done.1, bf16[8,256,256]{1,2,0:T(8,128)(2,1)S(1)} %bitcast_select_fusion, bf16[3,256,256]{1,2,0:T(8,128)(2,1)} %copy-done.2), kind=kLoop, calls=%fused_computation.13 | loop fusion | flops 1835008 | bytes 3670016 | tf_op jit(solution)/shard_map/concatenate | solution.py:18
  79.7 5.2 %gather_fusion = bf16[56,256,256]{1,2,0:T(8,128)(2,1)} fusion(bf16[14,256,256]{1,2,0:T(8,128)(2,1)S(1)} %pad_maximum_fusion, s32[1024]{0:T(1024)S(1)} %pad_clamp_fusion.2), kind=kCustom, calls=%fused_computation | custom fusion | bytes 14680288 | tf_op jit(solution)/shard_map/gather | solution.py:55
  84.9 8.6 %fusion.12 = bf16[1,8,256,256]{2,3,1,0:T(8,128)(2,1)S(1)} fusion(f32[8,256,256]{1,2,0:T(8,128)} %copy.38, f32[256,8,256]{2,0,1:T(8,128)} %fusion.21, bf16[1,8,7,256,256]{4,3,2,1,0:T(8,128)(2,1)} %param.19, bf16[8,7,256,256]{2,3,1,0:T(8,128)(2,1)} %bitcast.102, pred[8,7]{1,0:T(8,128)(4,1)S(1)} %copy-done.9, pred[8,256]{1,0:T(8,128)(4,1)S(1)} %tile.9), kind=kOutput, calls=%fused_computation.14 | convolution fusion | flops 1884815360 | bytes 19925048 | tf_op jit(solution)/shard_map/lsij,lsjn->lin/dot_general | solution.py:59
  93.5 1.3 %copy.39 = bf16[1,8,256,256]{3,2,1,0:T(8,128)(2,1)} copy(bf16[1,8,256,256]{2,3,1,0:T(8,128)(2,1)S(1)} %fusion.12) | data formatting | bytes 2097152 | tf_op jit(solution)/shard_map/broadcast_in_dim | solution.py:119
  (59 shorter events, 9.9 us)
Async XLA Ops:
  0.0 35.1 %copy-start = (bf16[1,8,256,128]{3,2,1,0:T(8,128)(2,1)S(1)}, bf16[1,8,256,128]{3,2,1,0:T(8,128)(2,1)}, u32[]{:S(2)}) copy-start(bf16[1,8,256,128]{3,2,1,0:T(8,128)(2,1)} %param.24) | copy-start | bytes 1572868
  2.2 0.9 copy-start.5
  2.3 5.9 %copy-start.1 = (bf16[1,8,256,256]{3,2,1,0:T(8,128)(2,1)S(1)}, bf16[1,8,256,256]{3,2,1,0:T(8,128)(2,1)}, u32[]{:S(2)}) copy-start(bf16[1,8,256,256]{3,2,1,0:T(8,128)(2,1)} %param.15) | copy-start | bytes 3145732
  4.9 34.5 %collective-permute-start.2 = (bf16[2,1,16,4,256]{4,3,2,1,0:T(4,128)(2,1)}, bf16[2,1,16,4,256]{4,3,2,1,0:T(4,128)(2,1)}, u32[]{:S(2)}, u32[]{:S(2)}) collective-permute-start(bf16[2,1,16,4,256]{4,3,2,1,0:T(4,128)(2,1)} %get-tuple-element.11), channel_id=1, source_target_pairs={{0,1},{1,0},{2,3},{3,2},{4,5},{5,4},{6,7},{7,6},{8,9},{9,8},{10,11... | collective-permute-start | bytes 196616 | tf_op jit(solution)/shard_map/ppermute | solution.py:92
  6.9 33.3 %collective-permute-start.3 = (bf16[2,1,16,4,256]{4,3,2,1,0:T(4,128)(2,1)}, bf16[2,1,16,4,256]{4,3,2,1,0:T(4,128)(2,1)}, u32[]{:S(2)}, u32[]{:S(2)}) collective-permute-start(bf16[2,1,16,4,256]{4,3,2,1,0:T(4,128)(2,1)} %get-tuple-element.10), channel_id=1, source_target_pairs={{0,2},{1,3},{2,0},{3,1},{4,6},{5,7},{6,4},{7,5},{8,10},{9,11},{10,... | collective-permute-start | bytes 196616 | tf_op jit(solution)/shard_map/ppermute | solution.py:92
  8.2 33.0 %collective-permute-start.4 = (bf16[2,1,16,4,256]{4,3,2,1,0:T(4,128)(2,1)}, bf16[2,1,16,4,256]{4,3,2,1,0:T(4,128)(2,1)}, u32[]{:S(2)}, u32[]{:S(2)}) collective-permute-start(bf16[2,1,16,4,256]{4,3,2,1,0:T(4,128)(2,1)} %get-tuple-element.9), channel_id=1, source_target_pairs={{0,3},{1,2},{2,1},{3,0},{4,7},{5,6},{6,5},{7,4},{8,11},{9,10},{10,... | collective-permute-start | bytes 196616 | tf_op jit(solution)/shard_map/ppermute | solution.py:92
  8.7 4.9 %copy-start.7 = (s32[1,1,2,4]{3,2,1,0:T(2,128)S(1)}, s32[1,1,2,4]{3,2,1,0:T(2,128)}, u32[]{:S(2)}) copy-start(s32[1,1,2,4]{3,2,1,0:T(2,128)} %param.27) | copy-start | bytes 100
  8.7 5.7 %copy-start.3 = (f32[1,1,2,4,16]{4,3,2,1,0:T(4,128)S(1)}, f32[1,1,2,4,16]{4,3,2,1,0:T(4,128)}, u32[]{:S(2)}) copy-start(f32[1,1,2,4,16]{4,3,2,1,0:T(4,128)} %param.28) | copy-start | bytes 1540
  8.9 25.6 %copy-start.6 = (s32[1,8,7]{1,0,2:T(1,128)S(1)}, s32[1,8,7]{1,0,2:T(1,128)}, u32[]{:S(2)}) copy-start(s32[1,8,7]{1,0,2:T(1,128)} %param.17) | copy-start | bytes 676
  9.0 68.6 %collective-permute-start = (bf16[3,256,256]{1,2,0:T(8,128)(2,1)S(1)}, bf16[3,256,256]{1,2,0:T(8,128)(2,1)S(1)}, u32[]{:S(2)}, u32[]{:S(2)}) collective-permute-start(bf16[3,256,256]{1,2,0:T(8,128)(2,1)S(1)} %get-tuple-element.5), channel_id=1, source_target_pairs={{0,1},{1,2},{2,3},{4,5},{5,6},{6,7},{8,9},{9,10},{10,11},{12,13},{... | collective-permute-start | bytes 1179656 | tf_op jit(solution)/shard_map/ppermute | solution.py:14
  12.3 66.0 %collective-permute-start.1 = (bf16[3,256,256]{1,2,0:T(8,128)(2,1)S(1)}, bf16[3,256,256]{1,2,0:T(8,128)(2,1)}, u32[]{:S(2)}, u32[]{:S(2)}) collective-permute-start(bf16[3,256,256]{1,2,0:T(8,128)(2,1)S(1)} %get-tuple-element.6), channel_id=1, source_target_pairs={{1,0},{2,1},{3,2},{5,4},{6,5},{7,6},{9,8},{10,9},{11,10},{13,12},{... | collective-permute-start | bytes 1179656 | tf_op jit(solution)/shard_map/ppermute | solution.py:17
  16.4 22.8 %copy-start.4 = (s32[1,1,2,4,16]{4,3,2,1,0:T(4,128)S(1)}, s32[1,1,2,4,16]{4,3,2,1,0:T(4,128)}, u32[]{:S(2)}) copy-start(s32[1,1,2,4,16]{4,3,2,1,0:T(4,128)} %param.26) | copy-start | bytes 1540
  35.1 20.1 %copy-start.8 = (f32[4]{0:T(128)S(1)}, f32[4]{0:T(128)}, u32[]{:S(2)}) copy-start(f32[4]{0:T(128)} %constant.4.clone) | copy-start | bytes 52
  42.1 8.7 %collective-permute-start.5 = (bf16[4,16,4,256]{3,2,1,0:T(4,128)(2,1)S(1)}, bf16[4,16,4,256]{3,2,1,0:T(4,128)(2,1)S(1)}, u32[]{:S(2)}, u32[]{:S(2)}) collective-permute-start(bf16[4,16,4,256]{3,2,1,0:T(4,128)(2,1)S(1)} %get-tuple-element.7), channel_id=1, source_target_pairs={{0,4},{4,8},{8,12},{12,16},{16,20},{20,24},{24,28},{1,5},{5,9},{9,... | collective-permute-start | bytes 393224 | tf_op jit(solution)/shard_map/ppermute | solution.py:25
  48.8 6.3 %collective-permute-start.6 = (bf16[4,16,4,256]{3,2,1,0:T(4,128)(2,1)S(1)}, bf16[4,16,4,256]{3,2,1,0:T(4,128)(2,1)S(1)}, u32[]{:S(2)}, u32[]{:S(2)}) collective-permute-start(bf16[4,16,4,256]{3,2,1,0:T(4,128)(2,1)S(1)} %get-tuple-element.8), channel_id=1, source_target_pairs={{4,0},{8,4},{12,8},{16,12},{20,16},{24,20},{28,24},{5,1},{9,5},{13... | collective-permute-start | bytes 393224 | tf_op jit(solution)/shard_map/ppermute | solution.py:25
  77.6 0.7 copy-start.2
  79.7 5.3 %copy-start.9 = (pred[8,7]{1,0:T(8,128)(4,1)S(1)}, pred[8,7]{1,0:T(8,128)(4,1)}, u32[]{:S(2)}) copy-start(pred[8,7]{1,0:T(8,128)(4,1)} %iota_compare_fusion.1) | copy-start | bytes 172
